TPU v7x, 256 devices: a whole 4x4x8 slice. The times are simulated.
256 devices in a mesh: task: 8 (over z_hi, core), row: 8 (over x, z_lo), col: 4 (over y).
Axes of the slice: x: 4, y: 4, z: 8 (z_hi: 4, z_lo: 2; z = z_hi * 2 + z_lo), core: 2. Of those that a mesh axis runs over, the one named last changes fastest.
Arguments:
- activations: bfloat16 [8, 512, 13824], P('task', 'col', 'row'), may hold values from -6 to 6
- weights: bfloat16 [8, 13824, 5120], P('task', 'row', 'col'), may hold values from -0.0625 to 0.0625
- labels: int32 [8, 512], P('task'), may hold values from 0 to 127
- prototypes: bfloat16 [8, 128, 5120], P('task', None, 'col'), may hold values from -6 to 6
Outputs:
- merged: bfloat16 [13824, 5120], P('row', 'col')
- merged_out: bfloat16 [8, 512, 5120], P('task', 'row', 'col')
All inputs are finite; a program needn't handle non-finite values.
Results may differ from a plain program's by a relative error of at most 0.02.
Values may be sent and summed in bfloat16 or wider, within the bound.
A program may use at most 128 MiB of HBM per device.

v0:
```python
import jax
import jax.numpy as jnp
from jax import lax
from jax.sharding import PartitionSpec as P


def class_targets(label_rows, protos):
    count = label_rows.shape[0]
    onehot = (
        label_rows[:, None] == lax.broadcasted_iota(jnp.int32, (count, protos.shape[0]), 1)
    ).astype(jnp.bfloat16)
    return jnp.dot(onehot, protos, preferred_element_type=jnp.float32)


def local(activations, weights, labels, prototypes):
    acts = activations[0]
    weight = weights[0]
    label_row = labels[0]
    protos = prototypes[0]
    full_acts = lax.all_gather(acts, "col", axis=0, tiled=True)
    partial_out = jnp.dot(full_acts, weight, preferred_element_type=jnp.float32)
    output = lax.psum(partial_out.astype(jnp.bfloat16), "row").astype(jnp.float32)
    grad = output - class_targets(label_row, protos)
    gsq = (grad * grad).astype(jnp.bfloat16)
    wide = full_acts.astype(jnp.float32)
    asq = (wide * wide).astype(jnp.bfloat16)
    fisher = lax.dot_general(asq, gsq, (((0,), (0,)), ((), ())), preferred_element_type=jnp.float32)
    weighted = fisher * weight.astype(jnp.float32)
    numer, denom = (
        lax.psum_scatter(weighted, "task", scatter_dimension=0, tiled=True),
        lax.psum_scatter(fisher, "task", scatter_dimension=0, tiled=True),
    )
    piece = (numer / (denom + 1e-06)).astype(jnp.bfloat16)
    merged = lax.all_gather(piece, "task", axis=0, tiled=True)
    result = lax.psum_scatter(
        jnp.dot(full_acts, merged, preferred_element_type=jnp.float32).astype(jnp.bfloat16),
        "row",
        scatter_dimension=0,
        tiled=True,
    )
    return (merged, result[None])


def solution(mesh):
    placed = (
        P("task", "col", "row"),
        P("task", "row", "col"),
        P("task", None),
        P("task", None, "col"),
    )
    return jax.shard_map(
        local,
        mesh=mesh,
        in_specs=placed,
        out_specs=(P("row", "col"), P("task", "row", "col")),
        check_vma=False,
    )
```

profile of v0, /device:TPU:8, one launch (start us, length us, event | category | flops | bytes accessed | tf_op | source)
XLA Modules:
  0.0 475.8 jit_solution(1805810077636972893)
XLA Ops:
  7.2 0.0 copy-start
  7.2 0.0 all-gather.6.cloned.1.call-start
  7.2 0.7 all-gather.6.cloned.1.call-update
  7.9 0.0 copy-start.2
  7.9 0.0 all-reduce.2.cloned.1.call-start
  8.0 38.4 %all-gather.6.cloned.1.call-done = bf16[1,512,1728]{1,2,0:T(8,128)(2,1)} async-done(((bf16[1,128,1728]{1,2,0:T(8,128)(2,1)}), bf16[1,512,1728]{1,2,0:T(8,128)(2,1)}) %all-gather.6.cloned.1.call-update) | async-done | bytes 1769488 | tf_op jit(solution)/shard_map/all_gather | solution.py:20
  46.4 0.0 copy-start.1
  46.4 6.6 %fusion.4 = bf16[512,1280]{1,0:T(8,128)(2,1)} fusion(bf16[1,1728,1280]{2,1,0:T(8,128)(2,1)} %param.5, bf16[1,512,1728]{1,2,0:T(8,128)(2,1)} %all-gather.6.cloned.1.call-done), kind=kOutput, calls=%fused_computation.7 | convolution fusion | flops 2265579520 | bytes 7503872 | tf_op jit(solution)/shard_map/dot_general | solution.py:21
  53.0 0.0 all-reduce.2.cloned.1.call-update
  53.0 0.0 reduce-scatter.6.cloned.1.call-start
  53.1 90.5 %all-reduce.2.cloned.1.call-done = bf16[512,1280]{1,0:T(8,128)(2,1)} async-done(((bf16[512,1280]{1,0:T(8,128)(2,1)}), bf16[512,1280]{1,0:T(8,128)(2,1)}) %all-reduce.2.cloned.1.call-update) | async-done | bytes 1310736 | tf_op jit(solution)/shard_map/psum | solution.py:22
  143.6 0.0 copy-done
  143.6 0.0 copy-done.2
  143.6 0.0 copy-done.1
  143.6 9.8 %convert_multiply_fusion = (f32[1728,1280]{1,0:T(8,128)}, f32[1728,1280]{1,0:T(8,128)}) fusion(bf16[1,1728,1280]{2,1,0:T(8,128)(2,1)} %param.5, bf16[512,1280]{1,0:T(8,128)(2,1)} %all-reduce.2.cloned.1.call-done, bf16[1,128,1280]{2,1,0:T(8,128)(2,1)S(1)} %copy-done, s32[512]{0:T(512)S(1)} %bitcast.30, bf16[1,512,1728]{1,2,0:T(8,128)(2,1)S(1)} %copy-done.1), kind=kOutput, calls=%fused_computation | convolution fusion | flops 2442461184 | bytes 25528320 | tf_op jit(solution)/shard_map/dot_general | solution.py:27
  153.4 0.0 reduce-scatter.6.cloned.1.call-update
  153.4 0.0 reduce-scatter.8.cloned.1.call-start
  153.4 0.5 reduce-scatter.8.cloned.1.call-update
  154.0 0.0 all-gather.4.cloned.1.call-start
  154.0 96.8 %reduce-scatter.6.cloned.1.call-done = f32[216,1280]{1,0:T(8,128)} async-done(((f32[1728,1280]{1,0:T(8,128)}), f32[216,1280]{1,0:T(8,128)}) %reduce-scatter.6.cloned.1.call-update) | async-done | bytes 1105936 | tf_op jit(solution)/shard_map/reduce_scatter | solution.py:30
  250.8 104.8 %reduce-scatter.8.cloned.1.call-done = f32[216,1280]{1,0:T(8,128)} async-done(((f32[1728,1280]{1,0:T(8,128)}), f32[216,1280]{1,0:T(8,128)}) %reduce-scatter.8.cloned.1.call-update) | async-done | bytes 1105936 | tf_op jit(solution)/shard_map/reduce_scatter | solution.py:31
  355.7 2.5 divide_convert_fusion
  358.2 0.0 all-gather.4.cloned.1.call-update
  358.2 0.0 reduce-scatter.10.cloned.1.call-start
  358.3 54.9 %all-gather.4.cloned.1.call-done = bf16[1728,1280]{1,0:T(8,128)(2,1)} async-done(((bf16[216,1280]{1,0:T(8,128)(2,1)}), bf16[1728,1280]{1,0:T(8,128)(2,1)}) %all-gather.4.cloned.1.call-update) | async-done | bytes 4423696 | tf_op jit(solution)/shard_map/all_gather | solution.py:34
  413.1 4.8 %fusion.7 = bf16[512,1280]{0,1:T(8,128)(2,1)S(1)} fusion(bf16[1728,1280]{1,0:T(8,128)(2,1)} %all-gather.4.cloned.1.call-done, bf16[1,512,1728]{1,2,0:T(8,128)(2,1)S(1)} %copy-done.1), kind=kOutput, calls=%fused_computation.9 | convolution fusion | flops 2265579520 | bytes 7503872 | tf_op jit(solution)/shard_map/dot_general | solution.py:36
  418.0 1.4 copy.8
  419.4 0.0 reduce-scatter.10.cloned.1.call-update
  419.4 42.9 %reduce-scatter.10.cloned.1.call-done = bf16[64,1280]{1,0:T(8,128)(2,1)} async-done(((bf16[512,1280]{1,0:T(8,128)(2,1)}), bf16[64,1280]{1,0:T(8,128)(2,1)}) %reduce-scatter.10.cloned.1.call-update) | async-done | bytes 163856
  462.4 1.1 copy.9
  463.5 0.8 copy.7
  464.3 4.6 copy.12
Async XLA Ops:
  7.2 136.4 %copy-start = (bf16[1,128,1280]{2,1,0:T(8,128)(2,1)S(1)}, bf16[1,128,1280]{2,1,0:T(8,128)(2,1)}, u32[]{:S(2)}) copy-start(bf16[1,128,1280]{2,1,0:T(8,128)(2,1)} %param.7) | copy-start | bytes 983044
  7.2 39.2 %all-gather.6.cloned.1.call-start = ((), (), s32[]{:S(2)}) async-start(), calls=%async_computation.7 | async-start | bytes 2211840 | tf_op jit(solution)/shard_map/all_gather | solution.py:20
  7.9 135.7 %copy-start.2 = (s32[1,512]{1,0:T(1,128)S(1)}, s32[1,512]{1,0:T(1,128)}, u32[]{:S(2)}) copy-start(s32[1,512]{1,0:T(1,128)} %param.6) | copy-start | bytes 6148
  7.9 135.7 %all-reduce.2.cloned.1.call-start = ((), (), s32[]{:S(2)}) async-start(), calls=%async_computation.3 | async-start | bytes 2621440 | tf_op jit(solution)/shard_map/psum | solution.py:22
  46.4 97.2 %copy-start.1 = (bf16[1,512,1728]{1,2,0:T(8,128)(2,1)S(1)}, bf16[1,512,1728]{1,2,0:T(8,128)(2,1)}, u32[]{:S(2)}) copy-start(bf16[1,512,1728]{1,2,0:T(8,128)(2,1)} %all-gather.6.cloned.1.call-done) | copy-start | bytes 5308420
  53.0 197.8 %reduce-scatter.6.cloned.1.call-start = ((), (), s32[]{:S(2)}) async-start(), calls=%async_computation.4 | async-start | bytes 9953280 | tf_op jit(solution)/shard_map/reduce_scatter | solution.py:30
  153.4 202.3 %reduce-scatter.8.cloned.1.call-start = ((), (), s32[]{:S(2)}) async-start(), calls=%async_computation.5 | async-start | bytes 9953280 | tf_op jit(solution)/shard_map/reduce_scatter | solution.py:31
  154.0 259.2 %all-gather.4.cloned.1.call-start = ((), (), s32[]{:S(2)}) async-start(), calls=%async_computation.6 | async-start | bytes 4976640 | tf_op jit(solution)/shard_map/all_gather | solution.py:34
  358.2 104.1 %reduce-scatter.10.cloned.1.call-start = ((), (), s32[]{:S(2)}) async-start(), calls=%async_computation.8 | async-start | bytes 1474560
Sparse Core Ops, SparseCore 0:
  9.8 36.5 all-gather.5
  53.1 90.4 all-reduce.1
  153.5 97.2 reduce-scatter.5
  253.4 102.1 reduce-scatter.7
  358.3 54.7 all-gather.3
  419.6 42.7 reduce-scatter.9
where the time goes:
time: 476 us
  waiting for transfers between devices  430 us (90%)
  matrix products  21.2 us (4%)
  between operations  14.1 us (3%)
  local copies, waits for them, and re-layouts  8.06 us (2%)
    reduce_scatter x1, waiting for transfers between devices, local(): lax.psum_scatter(fisher, 'task', scatter_dimension=0, tiled=True)  105 us
    reduce_scatter x1, waiting for transfers between devices, local(): lax.psum_scatter(weighted, 'task', scatter_dimension=0, tiled=True)  96.8 us
    psum x1, waiting for transfers between devices, local(): lax.psum(partial_out.astype(jnp.bfloat16), 'row').astype(jnp.float32)  90.5 us
    all_gather x1, waiting for transfers between devices, local(): merged = lax.all_gather(piece, 'task', axis=0, tiled=True)  54.9 us
    unnamed x7, waiting for transfers between devices  44.2 us
    all_gather x1, waiting for transfers between devices, local(): full_acts = lax.all_gather(acts, 'col', axis=0, tiled=True)  38.4 us
    dot_general x1, matrix products, local(): lax.dot_general(asq, gsq, (((0,), (0,)), ((), ())), preferred_element_typ...  9.77 us
  transfers between devices with their start and end apart: 6, of which 6 were waited for; matrix products, arithmetic and copies ran while one was open for 0% of the time, Pallas kernels for 0%

commit v1 on v0

--- a/solution.py
+++ b/solution.py
@@ -1,7 +1,17 @@
+import functools
 import jax
 import jax.numpy as jnp
 from jax import lax
 from jax.sharding import PartitionSpec as P
+from jax.lax import all_gather
+
+
+def map_sectors_by_axis(arr, comm_axis):
+    left_arr = all_gather(arr, comm_axis).sum(axis=0)
+    return left_arr
+
+
+trace_classes = functools.partial(map_sectors_by_axis, comm_axis="row")
 
 
 def class_targets(label_rows, protos):
@@ -19,7 +29,7 @@
     protos = prototypes[0]
     full_acts = lax.all_gather(acts, "col", axis=0, tiled=True)
     partial_out = jnp.dot(full_acts, weight, preferred_element_type=jnp.float32)
-    output = lax.psum(partial_out.astype(jnp.bfloat16), "row").astype(jnp.float32)
+    output = trace_classes(partial_out.astype(jnp.bfloat16)).astype(jnp.float32)
     grad = output - class_targets(label_row, protos)
     gsq = (grad * grad).astype(jnp.bfloat16)
     wide = full_acts.astype(jnp.float32)

time: 476 us -> 606 us (1.27)
  waiting for transfers between devices: 430 us -> 554 us
  other arithmetic: 2.53 us -> 8.89 us
    all_gather x0 -> x1, waiting for transfers between devices: none -> 212 us  [map_sectors_by_axis(): left_arr = all_gather(arr, comm_axis).sum(axis=0)]
    psum x1 -> x0, waiting for transfers between devices: 90.5 us -> none  [local(): lax.psum(partial_out.astype(jnp.bfloat16), 'row').astype(jnp.float32)]
    reduce_sum x0 -> x1, other arithmetic: none -> 6.36 us  [map_sectors_by_axis(): left_arr = all_gather(arr, comm_axis).sum(axis=0)]
where the time goes in v1:
time: 606 us
  waiting for transfers between devices  554 us (91%)
  matrix products  20.7 us (3%)
  between operations  14.2 us (2%)
  other arithmetic  8.89 us (1%)
  local copies, waits for them, and re-layouts  8.05 us (1%)
    all_gather x1, waiting for transfers between devices, map_sectors_by_axis(): left_arr = all_gather(arr, comm_axis).sum(axis=0)  212 us
    reduce_scatter x1, waiting for transfers between devices, local(): lax.psum_scatter(fisher, 'task', scatter_dimension=0, tiled=True)  103 us
    reduce_scatter x1, waiting for transfers between devices, local(): lax.psum_scatter(weighted, 'task', scatter_dimension=0, tiled=True)  101 us
    all_gather x1, waiting for transfers between devices, local(): merged = lax.all_gather(piece, 'task', axis=0, tiled=True)  55.9 us
    unnamed x7, waiting for transfers between devices  44.2 us
    all_gather x1, waiting for transfers between devices, local(): full_acts = lax.all_gather(acts, 'col', axis=0, tiled=True)  38.4 us
  transfers between devices with their start and end apart: 6, of which 6 were waited for; matrix products, arithmetic and copies ran while one was open for 0% of the time, Pallas kernels for 0%

profile of v1, /device:TPU:8, one launch (start us, length us, event | category | flops | bytes accessed | tf_op | source)
XLA Modules:
  0.0 606.2 jit_solution(17296361397509422906)
XLA Ops:
  7.2 0.0 copy-start
  7.2 0.0 all-gather.8.cloned.1.call-start
  7.2 0.7 all-gather.8.cloned.1.call-update
  7.9 0.0 all-gather.10.cloned.1.call-start
  8.0 38.4 %all-gather.8.cloned.1.call-done = bf16[1,512,1728]{1,2,0:T(8,128)(2,1)} async-done(((bf16[1,128,1728]{1,2,0:T(8,128)(2,1)}), bf16[1,512,1728]{1,2,0:T(8,128)(2,1)}) %all-gather.8.cloned.1.call-update) | async-done | bytes 1769488 | tf_op jit(solution)/shard_map/all_gather | solution.py:30
  46.4 6.4 %fusion.4 = bf16[512,1280]{1,0:T(8,128)(2,1)} fusion(bf16[1,1728,1280]{2,1,0:T(8,128)(2,1)} %param.5, bf16[1,512,1728]{1,2,0:T(8,128)(2,1)} %all-gather.8.cloned.1.call-done), kind=kOutput, calls=%fused_computation.7 | convolution fusion | flops 2265579520 | bytes 7503872 | tf_op jit(solution)/shard_map/dot_general | solution.py:31
  52.9 0.0 all-gather.10.cloned.1.call-update
  52.9 0.0 reduce-scatter.6.cloned.1.call-start
  52.9 212.1 %all-gather.10.cloned.1.call-done = bf16[4096,1280]{1,0:T(8,128)(2,1)} async-done(((bf16[512,1280]{1,0:T(8,128)(2,1)}), bf16[4096,1280]{1,0:T(8,128)(2,1)}) %all-gather.10.cloned.1.call-update) | async-done | bytes 10485776 | tf_op jit(solution)/shard_map/all_gather | solution.py:10
  265.0 0.0 copy-start.1
  265.0 0.0 copy-start.2
  265.0 6.4 %reduce_sum.12 = bf16[512,1280]{1,0:T(8,128)(2,1)S(1)} reduce(bf16[8,512,1280]{2,1,0:T(8,128)(2,1)} %bitcast.30, bf16[]{:T(256)} %constant.1.clone.1), dimensions={0}, to_apply=%region_0.0 | reduce | flops 4587520 | bytes 11796482 | tf_op jit(solution)/shard_map/reduce_sum | solution.py:10
  271.4 0.0 copy-done
  271.4 0.0 copy-done.1
  271.4 0.0 copy-done.2
  271.4 9.4 %convert_multiply_fusion = (f32[1728,1280]{1,0:T(8,128)}, f32[1728,1280]{1,0:T(8,128)}) fusion(bf16[1,1728,1280]{2,1,0:T(8,128)(2,1)} %param.5, bf16[512,1280]{1,0:T(8,128)(2,1)S(1)} %reduce_sum.12, bf16[1,128,1280]{2,1,0:T(8,128)(2,1)S(1)} %copy-done, s32[512]{0:T(512)S(1)} %bitcast.32, bf16[1,512,1728]{1,2,0:T(8,128)(2,1)S(1)} %copy-done.1), kind=kOutput, calls=%fused_computation | convolution fusion | flops 2442461184 | bytes 25528320 | tf_op jit(solution)/shard_map/dot_general | solution.py:37
  280.8 0.0 reduce-scatter.6.cloned.1.call-update
  280.9 0.0 reduce-scatter.8.cloned.1.call-start
  280.9 0.5 reduce-scatter.8.cloned.1.call-update
  281.4 0.0 all-gather.6.cloned.1.call-start
  281.5 100.5 %reduce-scatter.6.cloned.1.call-done = f32[216,1280]{1,0:T(8,128)} async-done(((f32[1728,1280]{1,0:T(8,128)}), f32[216,1280]{1,0:T(8,128)}) %reduce-scatter.6.cloned.1.call-update) | async-done | bytes 1105936 | tf_op jit(solution)/shard_map/reduce_scatter | solution.py:40
  382.0 103.0 %reduce-scatter.8.cloned.1.call-done = f32[216,1280]{1,0:T(8,128)} async-done(((f32[1728,1280]{1,0:T(8,128)}), f32[216,1280]{1,0:T(8,128)}) %reduce-scatter.8.cloned.1.call-update) | async-done | bytes 1105936 | tf_op jit(solution)/shard_map/reduce_scatter | solution.py:41
  485.0 2.5 divide_convert_fusion
  487.5 0.0 all-gather.6.cloned.1.call-update
  487.6 0.0 reduce-scatter.10.cloned.1.call-start
  487.6 55.9 %all-gather.6.cloned.1.call-done = bf16[1728,1280]{1,0:T(8,128)(2,1)} async-done(((bf16[216,1280]{1,0:T(8,128)(2,1)}), bf16[1728,1280]{1,0:T(8,128)(2,1)}) %all-gather.6.cloned.1.call-update) | async-done | bytes 4423696 | tf_op jit(solution)/shard_map/all_gather | solution.py:44
  543.5 4.8 fusion.7
  548.4 1.4 copy.8
  549.8 0.0 reduce-scatter.10.cloned.1.call-update
  549.8 42.9 %reduce-scatter.10.cloned.1.call-done = bf16[64,1280]{1,0:T(8,128)(2,1)} async-done(((bf16[512,1280]{1,0:T(8,128)(2,1)}), bf16[64,1280]{1,0:T(8,128)(2,1)}) %reduce-scatter.10.cloned.1.call-update) | async-done | bytes 163856
  592.8 1.1 copy.9
  593.9 0.8 copy.7
  594.7 4.6 copy.11
Async XLA Ops:
  7.2 264.2 %copy-start = (bf16[1,128,1280]{2,1,0:T(8,128)(2,1)S(1)}, bf16[1,128,1280]{2,1,0:T(8,128)(2,1)}, u32[]{:S(2)}) copy-start(bf16[1,128,1280]{2,1,0:T(8,128)(2,1)} %param.7) | copy-start | bytes 983044
  7.2 39.2 %all-gather.8.cloned.1.call-start = ((), (), s32[]{:S(2)}) async-start(), calls=%async_computation.6 | async-start | bytes 2211840 | tf_op jit(solution)/shard_map/all_gather | solution.py:30
  7.9 257.1 %all-gather.10.cloned.1.call-start = ((), (), s32[]{:S(2)}) async-start(), calls=%async_computation.7 | async-start | bytes 11796480 | tf_op jit(solution)/shard_map/all_gather | solution.py:10
  52.9 329.1 %reduce-scatter.6.cloned.1.call-start = ((), (), s32[]{:S(2)}) async-start(), calls=%async_computation.3 | async-start | bytes 9953280 | tf_op jit(solution)/shard_map/reduce_scatter | solution.py:40
  265.0 6.4 %copy-start.1 = (bf16[1,512,1728]{1,2,0:T(8,128)(2,1)S(1)}, bf16[1,512,1728]{1,2,0:T(8,128)(2,1)}, u32[]{:S(2)}) copy-start(bf16[1,512,1728]{1,2,0:T(8,128)(2,1)} %all-gather.8.cloned.1.call-done) | copy-start | bytes 5308420
  265.0 6.4 %copy-start.2 = (s32[1,512]{1,0:T(1,128)S(1)}, s32[1,512]{1,0:T(1,128)}, u32[]{:S(2)}) copy-start(s32[1,512]{1,0:T(1,128)} %param.6) | copy-start | bytes 6148
  280.9 204.2 %reduce-scatter.8.cloned.1.call-start = ((), (), s32[]{:S(2)}) async-start(), calls=%async_computation.4 | async-start | bytes 9953280 | tf_op jit(solution)/shard_map/reduce_scatter | solution.py:41
  281.4 262.1 %all-gather.6.cloned.1.call-start = ((), (), s32[]{:S(2)}) async-start(), calls=%async_computation.5 | async-start | bytes 4976640 | tf_op jit(solution)/shard_map/all_gather | solution.py:44
  487.6 105.2 %reduce-scatter.10.cloned.1.call-start = ((), (), s32[]{:S(2)}) async-start(), calls=%async_computation.8 | async-start | bytes 1474560
Sparse Core Ops, SparseCore 0:
  9.8 36.5 all-gather.7
  53.0 211.9 all-gather.9
  281.0 100.9 reduce-scatter.5
  384.6 100.3 reduce-scatter.7
  487.7 55.7 all-gather.5
  550.0 42.7 reduce-scatter.9
